TPU v7x, 32 devices: a whole 2x2x4 slice. The times are simulated.
32 devices in a mesh: dp: 4 (over z), row: 2 (over x), col: 4 (over y, core).
Axes of the slice: x: 2, y: 2, z: 4, core: 2. Of those that a mesh axis runs over, the one named last changes fastest.
Arguments:
- tokens: bfloat16 [768, 16384], P(('row', 'col'), 'dp'), may hold values from -6 to 6
- cotangent: bfloat16 [768, 16384], P(('row', 'col'), 'dp'), may hold values from -6 to 6
- holder_of: int32 [8, 4], replicated, may hold values from 0 to 3, each once within a row
- lengths: int32 [8, 4, 4], replicated, may hold values from 0 to 512, as said below
- input_gain: float32 [768], P(('row', 'col')), may hold values from 0.5 to 1.5
- input_shift: float32 [768], P(('row', 'col')), may hold values from -1.5 to 1.5
- attend_weight: bfloat16 [3, 768, 768], P(None, 'col', 'row'), may hold values from -0.21875 to 0.21875
- attend_bias: float32 [2, 768], P(None, 'col'), may hold values from -1.5 to 1.5
- mixed_gain: float32 [768], P('col'), may hold values from 0.5 to 1.5
- mixed_shift: float32 [768], P('col'), may hold values from -1.5 to 1.5
- output_weight: bfloat16 [768, 768], P('col', 'row'), may hold values from -0.375 to 0.375
- output_bias: float32 [768], P(('row', 'col')), may hold values from -1.5 to 1.5
- middle_gain: float32 [768], P(('row', 'col')), may hold values from 0.5 to 1.5
- middle_shift: float32 [768], P(('row', 'col')), may hold values from -1.5 to 1.5
- expand_weight: bfloat16 [768, 3072], P('row', 'col'), may hold values from -0.375 to 0.375
- expand_bias: float32 [3072], P('col'), may hold values from -1.5 to 1.5
- hidden_gain: float32 [3072], P('col'), may hold values from 0.5 to 1.5
- hidden_shift: float32 [3072], P('col'), may hold values from -1.5 to 1.5
- shrink_weight: bfloat16 [3072, 768], P('col', 'row'), may hold values from -0.1875 to 0.1875
- shrink_bias: float32 [768], P(('row', 'col')), may hold values from -1.5 to 1.5
Outputs:
- block_out: bfloat16 [768, 16384], P(('row', 'col'), 'dp')
- input_grad: bfloat16 [768, 16384], P(('row', 'col'), 'dp')
- input_gain_grad: float32 [768], P(('row', 'col'))
- input_shift_grad: float32 [768], P(('row', 'col'))
- attend_weight_grad: float32 [3, 768, 768], P(None, 'col', 'row')
- attend_bias_grad: float32 [2, 768], P(None, 'col')
- mixed_gain_grad: float32 [768], P('col')
- mixed_shift_grad: float32 [768], P('col')
- output_weight_grad: float32 [768, 768], P('col', 'row')
- output_bias_grad: float32 [768], P(('row', 'col'))
- middle_gain_grad: float32 [768], P(('row', 'col'))
- middle_shift_grad: float32 [768], P(('row', 'col'))
- expand_weight_grad: float32 [768, 3072], P('row', 'col')
- expand_bias_grad: float32 [3072], P('col')
- hidden_gain_grad: float32 [3072], P('col')
- hidden_shift_grad: float32 [3072], P('col')
- shrink_weight_grad: float32 [3072, 768], P('col', 'row')
- shrink_bias_grad: float32 [768], P(('row', 'col'))
Inputs may be any that keep to these rules, and one draw needn't show every extreme that they name: Each row of holder_of names every holder once. The 4 lengths of a unit add up to 512; a zero length is an empty slot; in every micro-batch one unit is a single sequence of 512 tokens.
All inputs are finite; a program needn't handle non-finite values.
Results may differ from a plain program's by a relative error of at most 0.017.
Values may be sent and summed in bfloat16 or wider, within the bound.
No kernel may reach another device: no remote copies, remote signals or barrier semaphores. Data moves between devices by JAX's collectives and lax.ppermute only.
A program may use at most 128 MiB of HBM per device.

v0:
```python
import math
import jax
import jax.numpy as jnp
from jax import lax
from jax.sharding import PartitionSpec as P

HEAD = 64
eps = 1e-05
masked_score = -1e30
f32 = jnp.float32
bf16 = jnp.bfloat16
RC = ("row", "col")


def mm(spec, a, b):
    return jnp.einsum(spec, a, b, preferred_element_type=f32)


def norm(v, gain, shift):
    mu = jnp.mean(v, axis=0, keepdims=True)
    d = v - mu
    r = lax.rsqrt(jnp.mean(d * d, axis=0, keepdims=True) + eps)
    vh = d * r
    return (vh * gain + shift, vh, r)


def norm_back(up, vh, r, gain):
    h = up * gain
    m1 = jnp.mean(h, axis=0, keepdims=True)
    m2 = jnp.mean(h * vh, axis=0, keepdims=True)
    return (
        r * (h - m1 - vh * m2),
        jnp.sum(up * vh, axis=1, keepdims=True),
        jnp.sum(up, axis=1, keepdims=True),
    )


def scores_of(q, k, visible):
    s = mm("hek,heq->hkq", k, q) * (1.0 / math.sqrt(HEAD))
    return jnp.where(visible[None], s, masked_score)


def body(
    tokens,
    cotangent,
    holder_of,
    lengths,
    input_gain,
    input_shift,
    attend_weight,
    attend_bias,
    mixed_gain,
    mixed_shift,
    output_weight,
    output_bias,
    middle_gain,
    middle_shift,
    expand_weight,
    expand_bias,
    hidden_gain,
    hidden_shift,
    shrink_weight,
    shrink_bias,
):
    holders = lax.axis_size("dp")
    half = holders // 2
    nr, nc = (lax.axis_size("row"), lax.axis_size("col"))
    n = nr * nc
    micro = holder_of.shape[0]
    assert micro == n
    fl = tokens.shape[0]
    pairs = micro * half
    blk = tokens.shape[1] // pairs
    unit = half * blk
    dp = lax.axis_index("dp")
    side, pos = (dp // half, dp % half)
    rc = lax.axis_index("row") * nc + lax.axis_index("col")
    groups = [[s * half + p for p in range(half)] for s in range(2)]

    def to_unit(v):
        v = v.reshape(fl, half, n, blk)
        v = jnp.transpose(v, (1, 2, 0, 3))
        v = lax.all_to_all(v, "dp", 0, 0, axis_index_groups=groups, tiled=True)
        v = jnp.transpose(v, (1, 2, 0, 3)).reshape(n, fl, unit)
        v = lax.all_to_all(v, RC, 0, 0, tiled=True)
        return v.reshape(n * fl, unit)

    def from_unit(v):
        v = lax.all_to_all(v.reshape(n, fl, unit), RC, 0, 0, tiled=True)
        v = jnp.transpose(v.reshape(n, fl, half, blk), (2, 0, 1, 3))
        v = lax.all_to_all(v, "dp", 0, 0, axis_index_groups=groups, tiled=True)
        return jnp.transpose(v, (2, 0, 1, 3)).reshape(tokens.shape)

    def gather(v):
        return lax.all_gather(v, RC, axis=0)

    ga = gather(attend_weight)
    go = gather(output_weight)
    ge = gather(expand_weight)
    gs = gather(shrink_weight)
    hw, rw, fw = (output_weight.shape[0], output_weight.shape[1], shrink_weight.shape[0])
    thin = jnp.concatenate(
        [
            v.reshape(-1)
            for v in (
                input_gain,
                input_shift,
                output_bias,
                middle_gain,
                middle_shift,
                shrink_bias,
                attend_bias,
                mixed_gain,
                mixed_shift,
                expand_bias,
                hidden_gain,
                hidden_shift,
            )
        ]
    )
    thin = lax.all_gather(thin, RC, axis=0)
    sizes = [fl] * 6 + [hw] * 4 + [fw] * 3
    cols, at = ([], 0)
    for i, size in enumerate(sizes):
        piece = thin[:, at : at + size] if i < 6 else thin[:nc, at : at + size]
        cols.append(piece.reshape(-1, 1))
        at += size
    in_g, in_s, out_b, mid_g, mid_s, shr_b, q_b, v_b, mix_g, mix_s, exp_b, hid_g, hid_s = cols
    k_unit = 2 * (pos * n + rc) + side
    m_of, u_of = (k_unit // holders, k_unit % holders)
    own = lengths[m_of, holder_of[m_of, u_of]]
    bounds = jnp.cumsum(own)[:-1]
    at_row = jnp.arange(unit, dtype=jnp.int32)
    segment = jnp.sum((at_row[:, None] >= bounds[None, :]).astype(jnp.int32), axis=1)
    visible = segment[:, None] == segment[None, :]
    x = to_unit(tokens).astype(f32)
    e2 = to_unit(cotangent)
    a, vh_in, r_in = norm(x, in_g, in_s)
    a = a.astype(bf16)
    gar = ga.reshape(nr, nc, 3, hw, rw)
    trip = mm("rcjif,rft->jcit", gar, a.reshape(nr, rw, unit)).reshape(3, nc * hw, unit)
    heads = lambda v: v.reshape(-1, HEAD, unit)
    q = heads((trip[0] + q_b).astype(bf16))
    k = heads(trip[1].astype(bf16))
    v = heads((trip[2] + v_b).astype(bf16))
    s = scores_of(q, k, visible)
    top = jnp.max(s, axis=1, keepdims=True)
    ex = jnp.exp(s - top)
    den = jnp.sum(ex, axis=1, keepdims=True)
    prob = ex / den
    o = mm("hek,hkq->heq", v, prob.astype(bf16)).reshape(nc * hw, unit)
    on, vh_mix, r_mix = norm(o, mix_g, mix_s)
    on = on.astype(bf16)
    gor = go.reshape(nr, nc * hw, rw)
    x1 = x + mm("rin,it->rnt", gor, on).reshape(nr * rw, unit) + out_b
    b, vh_mid, r_mid = norm(x1, mid_g, mid_s)
    b = b.astype(bf16)
    ger = ge.reshape(nr, nc, rw, fw)
    f = mm("rckn,rkt->cnt", ger, b.reshape(nr, rw, unit)).reshape(nc * fw, unit) + exp_b
    phi = 0.5 * (1.0 + lax.erf(f * math.sqrt(0.5)))
    g = f * phi
    gn, vh_hid, r_hid = norm(g, hid_g, hid_s)
    gn = gn.astype(bf16)
    gsr = gs.reshape(nr, nc * fw, rw)
    y = x1 + mm("rfn,ft->rnt", gsr, gn).reshape(nr * rw, unit) + shr_b
    block_out = from_unit(y.astype(bf16))
    e2r = e2.reshape(nr, rw, unit)
    d_shr_w = mm("cft,rdt->rcfd", gn.reshape(nc, fw, unit), e2r).astype(bf16)
    dy = e2.astype(f32)
    d_shr_b = jnp.sum(dy, axis=1, keepdims=True)
    dgn = mm("rfd,rdt->ft", gsr, e2r)
    dg, d_hid_g, d_hid_s = norm_back(dgn, vh_hid, r_hid, hid_g)
    slope = phi + f * (jnp.exp(-0.5 * f * f) * (1.0 / math.sqrt(2.0 * math.pi)))
    df = (dg * slope).astype(bf16)
    d_exp_b = jnp.sum(df.astype(f32), axis=1, keepdims=True)
    dfc = df.reshape(nc, fw, unit)
    d_exp_w = mm("rkt,cnt->rckn", b.reshape(nr, rw, unit), dfc).astype(bf16)
    db = mm("rckn,cnt->rkt", ger, dfc).reshape(nr * rw, unit)
    dx1, d_mid_g, d_mid_s = norm_back(db, vh_mid, r_mid, mid_g)
    dx1 = dy + dx1
    e1 = dx1.astype(bf16)
    d_out_b = jnp.sum(e1.astype(f32), axis=1, keepdims=True)
    e1r = e1.reshape(nr, rw, unit)
    d_out_w = mm("cit,rnt->rcin", on.reshape(nc, hw, unit), e1r).astype(bf16)
    don = mm("rin,rnt->it", gor, e1r)
    do, d_mix_g, d_mix_s = norm_back(don, vh_mix, r_mix, mix_g)
    do = heads(do.astype(bf16))
    dprob = mm("hek,heq->hkq", v, do)
    inner = jnp.sum(prob * dprob, axis=1, keepdims=True)
    ds = (prob * (dprob - inner)).astype(bf16)
    scale = 1.0 / math.sqrt(HEAD)
    dq = (mm("hek,hkq->heq", k, ds) * scale).astype(bf16).reshape(nc, hw, unit)
    dk = (mm("heq,hkq->hek", q, ds) * scale).astype(bf16).reshape(nc, hw, unit)
    dv = mm("heq,hkq->hek", do, prob.astype(bf16)).astype(bf16).reshape(nc, hw, unit)
    d_q_b = jnp.sum(dq.astype(f32), axis=2)
    d_v_b = jnp.sum(dv.astype(f32), axis=2)
    dtrip = jnp.stack([dq, dk, dv], axis=1)
    d_att_w = mm("cjit,rft->rcjif", dtrip, a.reshape(nr, rw, unit)).astype(bf16)
    da = mm("rcjif,cjit->rft", gar, dtrip).reshape(nr * rw, unit)
    dx, d_in_g, d_in_s = norm_back(da, vh_in, r_in, in_g)
    input_grad = from_unit((dx1 + dx).astype(bf16))

    def reduce(v):
        v = v.reshape((n,) + v.shape[2:])
        return lax.psum(lax.psum_scatter(v, RC, scatter_dimension=0, tiled=False), "dp")

    shr_w_g = reduce(d_shr_w).astype(f32)
    exp_w_g = reduce(d_exp_w).astype(f32)
    out_w_g = reduce(d_out_w).astype(f32)
    by_rc = [v.reshape(n, fl) for v in (d_in_g, d_in_s, d_out_b, d_mid_g, d_mid_s, d_shr_b)]
    by_c = [
        jnp.broadcast_to(v.reshape(1, nc, -1), (nr, nc, v.size // nc)).reshape(n, -1)
        for v in (d_q_b, d_v_b, d_mix_g, d_mix_s, d_exp_b, d_hid_g, d_hid_s)
    ]
    small = jnp.concatenate(by_rc + by_c, axis=1).astype(bf16)
    width = small.shape[1]
    pad = -width % rw
    small = jnp.pad(small, ((0, 0), (0, pad))).reshape(nr, nc, -1, rw)
    last = jnp.concatenate([d_att_w.reshape(nr, nc, 3 * hw, rw), small], axis=2)
    last = reduce(last).astype(f32)
    att_w_g = last[: 3 * hw].reshape(attend_weight.shape)
    flat = last[3 * hw :].reshape(-1)
    outs, at = ([], 0)
    for size in sizes:
        outs.append(flat[at : at + size])
        at += size
    (
        in_g_g,
        in_s_g,
        out_b_g,
        mid_g_g,
        mid_s_g,
        shr_b_g,
        q_b_g,
        v_b_g,
        mix_g_g,
        mix_s_g,
        exp_b_g,
        hid_g_g,
        hid_s_g,
    ) = outs
    return (
        block_out,
        input_grad,
        in_g_g,
        in_s_g,
        att_w_g,
        jnp.stack([q_b_g, v_b_g]),
        mix_g_g,
        mix_s_g,
        out_w_g,
        out_b_g,
        mid_g_g,
        mid_s_g,
        exp_w_g,
        exp_b_g,
        hid_g_g,
        hid_s_g,
        shr_w_g,
        shr_b_g,
    )


def solution(mesh):
    wide, narrow = (P(RC), P("col"))
    in_specs = (
        P(RC, "dp"),
        P(RC, "dp"),
        P(),
        P(),
        wide,
        wide,
        P(None, "col", "row"),
        P(None, "col"),
        narrow,
        narrow,
        P("col", "row"),
        wide,
        wide,
        wide,
        P("row", "col"),
        narrow,
        narrow,
        narrow,
        P("col", "row"),
        wide,
    )
    out_specs = (
        P(RC, "dp"),
        P(RC, "dp"),
        wide,
        wide,
        P(None, "col", "row"),
        P(None, "col"),
        narrow,
        narrow,
        P("col", "row"),
        wide,
        wide,
        wide,
        P("row", "col"),
        narrow,
        narrow,
        narrow,
        P("col", "row"),
        wide,
    )
    return jax.shard_map(body, mesh=mesh, in_specs=in_specs, out_specs=out_specs, check_vma=False)
```

profile of v0, /device:TPU:0, one launch (start us, length us, event | category | flops | bytes accessed | tf_op | source)
XLA Modules:
  0.0 607.2 jit_solution(13611442720965010342)
XLA Ops:
  15.2 4.3 all-to-all-start
  20.6 10.5 %all-to-all-done = bf16[2,8,96,256]{3,1,2,0:T(8,128)(2,1)S(1)} async-done(((bf16[2,8,96,256]{3,1,2,0:T(8,128)(2,1)}), bf16[2,8,96,256]{3,1,2,0:T(8,128)(2,1)S(1)}, u32[]{:S(2)}, u32[]{:S(2)}) %all-to-all-start) | async-done | bytes 786464 | tf_op jit(solution)/shard_map/all_to_all | solution.py:83
  48.9 18.1 %all-reduce.6.cloned.1.call-done = f32[29184]{0:T(1024)} async-done(((f32[29184]{0:T(1024)}), f32[29184]{0:T(1024)}) %all-reduce.6.cloned.1.call-update) | async-done | bytes 116752
  73.3 4.2 all-to-all-start.5
  78.7 32.7 %all-gather.10.cloned.1.call-done = bf16[24,192,384]{2,1,0:T(8,128)(2,1)} async-done(((bf16[3,192,384]{2,1,0:T(8,128)(2,1)}), bf16[24,192,384]{2,1,0:T(8,128)(2,1)}) %all-gather.10.cloned.1.call-update) | async-done | bytes 3538960 | tf_op jit(solution)/shard_map/all_gather | solution.py:95
  111.5 4.1 convolution_bitcast_fusion.1
  117.9 10.7 %fusion.64 = (f32[12,512]{1,0:T(8,128)S(1)}, f32[12,512,512]{2,1,0:T(8,128)}) fusion(pred[512,512]{1,0:T(8,128)(4,1)S(1)} %broadcast_compare_fusion, bf16[12,64,512]{2,1,0:T(8,128)(2,1)S(1)} %bitcast.299, f32[12,64,512]{2,1,0:T(8,128)} %bitcast.302, f32[12,64]{1,0:T(8,128)S(1)} %add.260), kind=kOutput, calls=%fused_computation.139 | convolution fusion | flops 416023040 | bytes 15232000 | tf_op jit(solution)/shard_map/sub | solution.py:148
  128.6 6.6 %fusion.65 = (f32[512]{0:T(512)S(1)}, f32[12,64,512]{2,1,0:T(8,128)S(1)}) fusion(f32[12,512,512]{2,1,0:T(8,128)} %get-tuple-element.76, f32[12,512]{1,0:T(8,128)S(1)} %get-tuple-element.75, f32[12,64,512]{2,1,0:T(8,128)} %bitcast.321, f32[12,64]{1,0:T(8,128)S(1)} %add.249), kind=kOutput, calls=%fused_computation.140 | convolution fusion | flops 410123776 | bytes 15758336 | tf_op jit(solution)/shard_map/hek,hkq->heq/dot_general | solution.py:16
  144.4 34.1 %all-gather.14.cloned.1.call-done = bf16[3072,768]{1,0:T(8,128)(2,1)} async-done(((bf16[384,768]{1,0:T(8,128)(2,1)}), bf16[3072,768]{1,0:T(8,128)(2,1)}) %all-gather.14.cloned.1.call-update) | async-done | bytes 4718608 | tf_op jit(solution)/shard_map/all_gather | solution.py:95
  178.5 9.2 %fusion.54 = (f32[512]{0:T(512)S(1)}, f32[4,768,512]{1,2,0:T(8,128)}, f32[4,768,512]{1,2,0:T(8,128)}) fusion(f32[4,768]{1,0:T(4,128)S(1)} %get-tuple-element.57, bf16[2,4,384,768]{3,2,1,0:T(8,128)(2,1)} %bitcast.344, f32[2,384]{1,0:T(2,128)S(1)} %add.275, f32[2,384]{1,0:T(2,128)S(1)} %mul.381, f32[512]{0:T(512)S(1)} %add_rsqrt_fusion.1, ...), kind=kOutput, calls=%fused_computation.130 | convolution fusion | flops 2427321856 | bytes 18898944 | tf_op jit(solution)/shard_map/rckn,rkt->cnt/dot_general | solution.py:16
  187.7 6.7 %copy.132 = f32[4,768,512]{2,1,0:T(8,128)} copy(f32[4,768,512]{1,2,0:T(8,128)} %get-tuple-element.79) | data formatting | bytes 12582912 | tf_op jit(solution)/shard_map/rckn,rkt->cnt/dot_general | solution.py:16
  197.9 21.4 %all-gather.16.cloned.1.call-done = bf16[6144,384]{1,0:T(8,128)(2,1)} async-done(((bf16[768,384]{1,0:T(8,128)(2,1)}), bf16[6144,384]{1,0:T(8,128)(2,1)}) %all-gather.16.cloned.1.call-update) | async-done | bytes 4718608 | tf_op jit(solution)/shard_map/all_gather | solution.py:95
  219.3 8.5 %fusion.8 = (bf16[3072]{0:T(1024)(128)(2,1)S(1)}, f32[512]{0:T(512)S(1)}, f32[512]{0:T(512)S(1)}, bf16[3072]{0:T(1024)(128)(2,1)S(1)}, f32[3072,512,1]{1,0,2:T(8,128)S(1)}) fusion(f32[4,768,512]{2,1,0:T(8,128)} %copy.132, f32[512]{0:T(512)S(1)} %broadcast_multiply_fusion.2, f32[3072]{0:T(1024)S(1)} %add.288, f32[512]{0:T(512)S(1)} %add_rsqrt_fusion, ...), kind=kOutput, calls=%fused_computation.17 | convolution fusion | flops 2437932032 | bytes 18132992 | tf_op jit(solution)/shard_map/rfd,rdt->ft/dot_general | solution.py:16
  227.9 7.7 %fusion.52 = (bf16[3072]{0:T(1024)(128)(2,1)S(1)}, bf16[3072,512]{1,0:T(8,128)(2,1)S(1)}) fusion(f32[512]{0:T(512)S(1)} %get-tuple-element.89, f32[512]{0:T(512)S(1)} %broadcast_multiply_fusion.2, f32[3072]{0:T(1024)S(1)} %add.288, f32[4,768,512]{2,1,0:T(8,128)S(1)} %bitcast.285, f32[512]{0:T(512)S(1)} %get-tuple-element.90, f32[3072]{0:T(1024)S(1)} %mul.396, ...), kind=kLoop, calls=%fused_computation.129 | loop fusion | flops 31454208 | bytes 15767552 | tf_op jit(solution)/shard_map/reduce_sum | solution.py:175
  235.6 6.0 fusion.30
  249.3 7.9 %fusion.67 = (bf16[12,64]{1,0:T(8,128)(2,1)S(1)}, bf16[12,64,512]{2,1,0:T(8,128)(2,1)}) fusion(bf16[12,64,512]{2,1,0:T(8,128)(2,1)} %bitcast.331, f32[12,512,512]{2,1,0:T(8,128)} %get-tuple-element.76, f32[12,512]{1,0:T(8,128)S(1)} %get-tuple-element.75), kind=kOutput, calls=%fused_computation.142 | convolution fusion | flops 409730304 | bytes 14181888 | tf_op jit(solution)/shard_map/heq,hkq->hek/dot_general | solution.py:16
  257.2 8.9 %multiply_reduce_fusion = (f32[12,512]{1,0:T(8,128)S(1)}, f32[12,512,512]{2,1,0:T(8,128)}) fusion(f32[12,512,512]{2,1,0:T(8,128)} %get-tuple-element.76, f32[12,512]{1,0:T(8,128)S(1)} %get-tuple-element.75, bf16[12,64,512]{2,1,0:T(8,128)(2,1)S(1)} %bitcast.332, f32[12,64,512]{2,1,0:T(8,128)S(1)} %bitcast.322, f32[12,64]{1,0:T(8,128)S(1)} %add.249), kind=kOutput, calls=%fused_computation.2 | convolution fusion | flops 412870656 | bytes 27577344 | tf_op jit(solution)/shard_map/hek,heq->hkq/dot_general | solution.py:16
  266.1 6.5 %multiply_convert_fusion = bf16[12,512,512]{2,1,0:T(8,128)(2,1)S(1)} fusion(f32[12,512,512]{2,1,0:T(8,128)} %get-tuple-element.84, f32[12,512]{1,0:T(8,128)S(1)} %get-tuple-element.83, f32[12,512,512]{2,1,0:T(8,128)S(1)} %bitcast.298, f32[12,512]{1,0:T(8,128)S(1)} %get-tuple-element.75), kind=kLoop, calls=%fused_computation.1 | loop fusion | flops 12582912 | bytes 31506432 | tf_op jit(solution)/shard_map/convert_element_type | solution.py:190
  279.4 6.0 fusion.22
  299.5 4.0 add_convert_fusion
  305.2 4.2 convert_bitcast_fusion
  313.4 7.2 %convert_bitcast_fusion.1 = bf16[2,4,384,768]{2,3,0,1:T(8,128)(2,1)} fusion(bf16[4,768,512,1]{2,1,3,0:T(8,128)(2,1)} %bitcast.317, f32[2,384,512]{2,1,0:T(8,128)S(1)} %copy-done.10, f32[2,384]{1,0:T(2,128)S(1)} %add.275, f32[2,384]{1,0:T(2,128)S(1)} %mul.381, f32[512]{0:T(512)S(1)} %add_rsqrt_fusion.1, f32[512]{0:T(512)S(1)} %broadcast_multiply_fusion.9), kind=kOutput, calls=%fused_computation.30 | convolution fusion | flops 2420244480 | bytes 9447424 | tf_op jit(solution)/shard_map/rkt,cnt->rckn/dot_general | solution.py:16
  320.7 6.7 %copy.143 = bf16[2,4,384,768]{3,2,1,0:T(8,128)(2,1)} copy(bf16[2,4,384,768]{2,3,0,1:T(8,128)(2,1)} %convert_bitcast_fusion.1) | data formatting | bytes 9437184 | tf_op jit(solution)/shard_map/convert_element_type | solution.py:177
  327.4 4.8 copy.126
  332.2 5.8 fusion.69
  341.3 20.6 %all_to_all.40 = bf16[8,96,512]{2,1,0:T(8,128)(2,1)S(1)} all-to-all(bf16[8,96,512]{2,1,0:T(8,128)(2,1)S(1)} %get-tuple-element.47), channel_id=1, replica_groups=mesh['dp'=4,'row'=2,'col'=4] {'row','col'}, dimensions={0} | all-to-all | bytes 1572864 | tf_op jit(solution)/shard_map/all_to_all | solution.py:89
  365.6 17.6 %reduce-scatter.5.cloned.1.call-done = bf16[1,586,384]{2,1,0:T(8,128)(2,1)} async-done(((bf16[8,586,384]{2,1,0:T(8,128)(2,1)}), bf16[1,586,384]{2,1,0:T(8,128)(2,1)}) %reduce-scatter.5.cloned.1.call-update) | async-done | bytes 450064 | tf_op jit(solution)/shard_map/reduce_scatter | solution.py:205
  383.1 57.8 %reduce-scatter.11.cloned.1.call-done = bf16[1,768,384]{2,1,0:T(8,128)(2,1)} async-done(((bf16[8,768,384]{2,1,0:T(8,128)(2,1)}), bf16[1,768,384]{2,1,0:T(8,128)(2,1)}) %reduce-scatter.11.cloned.1.call-update) | async-done | bytes 589840 | tf_op jit(solution)/shard_map/reduce_scatter | solution.py:205
  441.0 57.4 %reduce-scatter.9.cloned.1.call-done = bf16[1,384,768]{2,1,0:T(8,128)(2,1)} async-done(((bf16[8,384,768]{2,1,0:T(8,128)(2,1)}), bf16[1,384,768]{2,1,0:T(8,128)(2,1)}) %reduce-scatter.9.cloned.1.call-update) | async-done | bytes 589840 | tf_op jit(solution)/shard_map/reduce_scatter | solution.py:205
  504.9 26.5 %all-to-all-done.7 = bf16[2,8,96,256]{3,1,2,0:T(8,128)(2,1)S(1)} async-done(((bf16[2,8,96,256]{3,1,2,0:T(8,128)(2,1)}), bf16[2,8,96,256]{3,1,2,0:T(8,128)(2,1)S(1)}, u32[]{:S(2)}, u32[]{:S(2)}) %all-to-all-start.7) | async-done | bytes 786464 | tf_op jit(solution)/shard_map/all_to_all | solution.py:91
  536.2 15.9 %all-to-all-done.3 = bf16[2,8,96,256]{3,1,2,0:T(8,128)(2,1)S(1)} async-done(((bf16[2,8,96,256]{3,1,2,0:T(8,128)(2,1)}), bf16[2,8,96,256]{3,1,2,0:T(8,128)(2,1)S(1)}, u32[]{:S(2)}, u32[]{:S(2)}) %all-to-all-start.3) | async-done | bytes 786464 | tf_op jit(solution)/shard_map/all_to_all | solution.py:91
  553.3 38.6 %all-reduce.8.cloned.1.call-done = (bf16[586,384]{1,0:T(8,128)(2,1)}, bf16[192,384]{1,0:T(8,128)(2,1)}, bf16[384,768]{1,0:T(8,128)(2,1)}, bf16[768,384]{1,0:T(8,128)(2,1)}) async-done(((bf16[586,384]{1,0:T(8,128)(2,1)}, bf16[192,384]{1,0:T(8,128)(2,1)}, bf16[384,768]{1,0:T(8,128)(2,1)}, bf16[768,384]{1,0:T(8,128)(2,1)}), (bf16[586,384]{1,0:T(8,128)(2,1)}, bf16[192,384]{1,0:T(8,128)(2,1)}, ...) | async-done | bytes 1777168 | tf_op jit(solution)/shard_map/psum | solution.py:205
  (267 shorter events, 108.1 us)
Async XLA Ops:
  7.2 31.3 %copy-start = (s32[8,4,4]{0,2,1:T(4,128)S(1)}, s32[8,4,4]{0,2,1:T(4,128)}, u32[]{:S(2)}) copy-start(s32[8,4,4]{0,2,1:T(4,128)} %param.23) | copy-start | bytes 1540
  7.2 6.9 %copy-start.23 = (bf16[96,4096]{1,0:T(8,128)(2,1)S(1)}, bf16[96,4096]{1,0:T(8,128)(2,1)}, u32[]{:S(2)}) copy-start(bf16[96,4096]{1,0:T(8,128)(2,1)} %param.20) | copy-start | bytes 2359300
  7.2 59.8 %all-reduce.6.cloned.1.call-start = ((), (), s32[]{:S(2)}) async-start(), calls=%async_computation.20 | async-start | bytes 237568
  12.0 99.5 %all-gather.10.cloned.1.call-start = ((), (), s32[]{:S(2)}) async-start(), calls=%async_computation.16 | async-start | bytes 3981312 | tf_op jit(solution)/shard_map/all_gather | solution.py:95
  12.8 125.5 %all-gather.12.cloned.1.call-start = ((), (), s32[]{:S(2)}) async-start(), calls=%async_computation.17 | async-start | bytes 1327104 | tf_op jit(solution)/shard_map/all_gather | solution.py:95
  13.5 165.0 %all-gather.14.cloned.1.call-start = ((), (), s32[]{:S(2)}) async-start(), calls=%async_computation.18 | async-start | bytes 5308416 | tf_op jit(solution)/shard_map/all_gather | solution.py:95
  15.2 15.9 %all-to-all-start = ((bf16[2,8,96,256]{3,1,2,0:T(8,128)(2,1)}), bf16[2,8,96,256]{3,1,2,0:T(8,128)(2,1)S(1)}, u32[]{:S(2)}, u32[]{:S(2)}) async-start(bf16[2,8,96,256]{3,1,2,0:T(8,128)(2,1)} %copy.120), calls=%async_computation | async-start | bytes 1572864 | tf_op jit(solution)/shard_map/all_to_all | solution.py:83
  31.1 14.0 %all-to-all-start.4 = ((bf16[2,8,96,256]{3,1,2,0:T(8,128)(2,1)}), bf16[2,8,96,256]{3,1,2,0:T(8,128)(2,1)S(1)}, u32[]{:S(2)}, u32[]{:S(2)}) async-start(bf16[2,8,96,256]{3,1,2,0:T(8,128)(2,1)} %copy.130), calls=%async_computation.4 | async-start | bytes 1572864 | tf_op jit(solution)/shard_map/all_to_all | solution.py:83
  34.6 184.7 %all-gather.16.cloned.1.call-start = ((), (), s32[]{:S(2)}) async-start(), calls=%async_computation.19 | async-start | bytes 5308416 | tf_op jit(solution)/shard_map/all_gather | solution.py:95
  45.1 28.2 %all-to-all-start.1 = ((bf16[8,96,512]{2,1,0:T(8,128)(2,1)}), bf16[8,96,512]{2,1,0:T(8,128)(2,1)S(1)}, u32[]{:S(2)}, u32[]{:S(2)}) async-start(bf16[8,96,512]{2,1,0:T(8,128)(2,1)} %reshape.770), calls=%async_computation.1 | async-start | bytes 1572864 | tf_op jit(solution)/shard_map/all_to_all | solution.py:85
  69.4 9.0 %copy-start.46 = (f32[2,384]{1,0:T(2,128)}, f32[2,384]{1,0:T(2,128)S(1)}, u32[]{:S(2)}) copy-start(f32[2,384]{1,0:T(2,128)S(1)} %mul.364) | copy-start | bytes 9220
  73.3 124.6 %all-to-all-start.5 = ((bf16[8,96,512]{2,1,0:T(8,128)(2,1)}), bf16[8,96,512]{2,1,0:T(8,128)(2,1)}, u32[]{:S(2)}, u32[]{:S(2)}) async-start(bf16[8,96,512]{2,1,0:T(8,128)(2,1)} %reshape.782), calls=%async_computation.5 | async-start | bytes 1572864 | tf_op jit(solution)/shard_map/all_to_all | solution.py:85
  77.5 288.0 %reduce-scatter.7.cloned.1.call-start = ((), (), s32[]{:S(2)}) async-start(), calls=%async_computation.13 | async-start | bytes 1327104 | tf_op jit(solution)/shard_map/reduce_scatter | solution.py:205
  78.4 37.2 %copy-start.44 = (f32[512]{0:T(512)}, f32[512]{0:T(512)S(1)}, u32[]{:S(2)}) copy-start(f32[512]{0:T(512)S(1)} %add_rsqrt_fusion.3) | copy-start | bytes 6148
  78.7 32.8 %copy-start.26 = (bf16[2,384,512,1,1]{2,1,4,3,0:T(8,128)(2,1)}, bf16[2,384,512,1,1]{2,1,4,3,0:T(8,128)(2,1)S(1)}, u32[]{:S(2)}) copy-start(bf16[2,384,512,1,1]{2,1,4,3,0:T(8,128)(2,1)S(1)} %fusion.41) | copy-start | bytes 2359300
  219.3 8.5 %slice-start = ((s8[6291456]{0:T(1024)(128)(4,1)}), s8[4194304]{0:T(1024)(128)(4,1)S(1)}, s32[]{:S(2)}) async-start(s8[6291456]{0:T(1024)(128)(4,1)} %bitcast.284), calls=%async_computation.22 | async-start | bytes 8388608
  219.3 8.5 %slice-start.1 = ((s8[6291456]{0:T(1024)(128)(4,1)}), s8[2097152]{0:T(1024)(128)(4,1)S(1)}, s32[]{:S(2)}) async-start(s8[6291456]{0:T(1024)(128)(4,1)} %bitcast.284), calls=%async_computation.23 | async-start | bytes 4194304
  227.9 7.8 %copy-start.9 = (f32[2,384,512]{2,1,0:T(8,128)S(1)}, f32[2,384,512]{2,1,0:T(8,128)}, u32[]{:S(2)}) copy-start(f32[2,384,512]{2,1,0:T(8,128)} %copy-done.8) | copy-start | bytes 4718596
  235.6 6.1 copy-start.17
  249.3 7.9 %copy-start.19 = (f32[1,4,192,512]{3,2,0,1:T(8,128)S(1)}, f32[1,4,192,512]{3,2,0,1:T(8,128)}, u32[]{:S(2)}) copy-start(f32[1,4,192,512]{3,2,0,1:T(8,128)} %get-tuple-element.46) | copy-start | bytes 4718596
  249.3 7.9 %copy-start.25 = (bf16[768,512]{1,0:T(8,128)(2,1)S(1)}, bf16[768,512]{1,0:T(8,128)(2,1)}, u32[]{:S(2)}) copy-start(bf16[768,512]{1,0:T(8,128)(2,1)} %copy.135) | copy-start | bytes 2359300
  249.3 16.8 %slice-start.2 = ((s8[12582912]{0:T(1024)(128)(4,1)}), s8[4194304]{0:T(1024)(128)(4,1)S(1)}, s32[]{:S(2)}) async-start(s8[12582912]{0:T(1024)(128)(4,1)} %bitcast.297), calls=%async_computation.24 | async-start | bytes 8388608
  249.3 16.8 %slice-start.3 = ((s8[12582912]{0:T(1024)(128)(4,1)}), s8[4194304]{0:T(1024)(128)(4,1)S(1)}, s32[]{:S(2)}) async-start(s8[12582912]{0:T(1024)(128)(4,1)} %bitcast.297), calls=%async_computation.25 | async-start | bytes 8388608
  257.2 8.9 %slice-start.4 = ((s8[12582912]{0:T(1024)(128)(4,1)}), s8[4194304]{0:T(1024)(128)(4,1)S(1)}, s32[]{:S(2)}) async-start(s8[12582912]{0:T(1024)(128)(4,1)} %bitcast.297), calls=%async_computation.26 | async-start | bytes 8388608
  266.1 6.5 %copy-start.15 = (f32[1,4,192,512]{3,2,0,1:T(8,128)S(1)}, f32[1,4,192,512]{3,2,0,1:T(8,128)}, u32[]{:S(2)}) copy-start(f32[1,4,192,512]{3,2,0,1:T(8,128)} %get-tuple-element.45) | copy-start | bytes 4718596
  279.4 103.8 %reduce-scatter.5.cloned.1.call-start = ((), (), s32[]{:S(2)}) async-start(), calls=%async_computation.12 | async-start | bytes 4091904 | tf_op jit(solution)/shard_map/reduce_scatter | solution.py:205
  298.8 142.2 %reduce-scatter.11.cloned.1.call-start = ((), (), s32[]{:S(2)}) async-start(), calls=%async_computation.15 | async-start | bytes 5308416 | tf_op jit(solution)/shard_map/reduce_scatter | solution.py:205
  312.0 186.3 %reduce-scatter.9.cloned.1.call-start = ((), (), s32[]{:S(2)}) async-start(), calls=%async_computation.14 | async-start | bytes 5308416 | tf_op jit(solution)/shard_map/reduce_scatter | solution.py:205
  361.9 137.9 %all-to-all-start.2 = ((bf16[8,96,512]{2,1,0:T(8,128)(2,1)}), bf16[8,96,512]{2,1,0:T(8,128)(2,1)S(1)}, u32[]{:S(2)}, u32[]{:S(2)}) async-start(bf16[8,96,512]{2,1,0:T(8,128)(2,1)} %get-tuple-element.48), calls=%async_computation.2 | async-start | bytes 1572864 | tf_op jit(solution)/shard_map/all_to_all | solution.py:89
  365.5 226.4 %all-reduce.8.cloned.1.call-start = ((), (), s32[]{:S(2)}) async-start(), calls=%async_computation.21 | async-start | bytes 3563520 | tf_op jit(solution)/shard_map/psum | solution.py:205
  499.9 31.5 %all-to-all-start.7 = ((bf16[2,8,96,256]{3,1,2,0:T(8,128)(2,1)}), bf16[2,8,96,256]{3,1,2,0:T(8,128)(2,1)S(1)}, u32[]{:S(2)}, u32[]{:S(2)}) async-start(bf16[2,8,96,256]{3,1,2,0:T(8,128)(2,1)} %copy.140), calls=%async_computation.7 | async-start | bytes 1572864 | tf_op jit(solution)/shard_map/all_to_all | solution.py:91
  531.4 20.7 %all-to-all-start.3 = ((bf16[2,8,96,256]{3,1,2,0:T(8,128)(2,1)}), bf16[2,8,96,256]{3,1,2,0:T(8,128)(2,1)S(1)}, u32[]{:S(2)}, u32[]{:S(2)}) async-start(bf16[2,8,96,256]{3,1,2,0:T(8,128)(2,1)} %copy.128), calls=%async_computation.3 | async-start | bytes 1572864 | tf_op jit(solution)/shard_map/all_to_all | solution.py:91
  (40 other events, 109.2 us)
Sparse Core Ops, SparseCore 0:
  12.1 54.8 all-reduce.5
  69.1 42.3 all-gather.9
  113.5 24.0 all-gather.11
  139.5 38.9 all-gather.13
  180.4 38.9 all-gather.15
  279.5 36.7 reduce-scatter.6
  319.8 63.2 reduce-scatter.4
  387.0 53.9 reduce-scatter.10
  444.4 53.8 reduce-scatter.8
  501.0 90.8 all-reduce.7
where the time goes:
time: 613 us; the launch traced here: 607 us
  waiting for transfers between devices  337 us (55%)
  matrix products  99.4 us (16%)
  local copies, waits for them, and re-layouts  60.3 us (10%)
  other arithmetic  45 us (7%)
  starting transfers between devices  26.8 us (4%)
  blocking collectives  20.6 us (3%)
  between operations  17.9 us (3%)
    reduce_scatter x4, waiting for transfers between devices, reduce(): lax.psum_scatter(v, RC, scatter_dimension=0, tiled=False)  133 us
    dot_general x17, matrix products, mm(): return jnp.einsum(spec, a, b, preferred_element_type=f32)  88.7 us
    all_gather x4, waiting for transfers between devices, gather(): return lax.all_gather(v, RC, axis=0)  88.3 us
    all_to_all x2, waiting for transfers between devices, from_unit(): v = lax.all_to_all(v, 'dp', 0, 0, axis_index_groups=groups, tiled=True)  42.4 us
    psum x1, waiting for transfers between devices, reduce(): lax.psum(lax.psum_scatter(v, RC, scatter_dimension=0, tiled=False), 'dp')  38.6 us
    unnamed x11, waiting for transfers between devices  20.7 us
    all_to_all x1, blocking collectives, from_unit(): v = lax.all_to_all(v.reshape(n, fl, unit), RC, 0, 0, tiled=True)  20.6 us
    all_to_all x2, waiting for transfers between devices, to_unit(): v = lax.all_to_all(v, 'dp', 0, 0, axis_index_groups=groups, tiled=True)  14.4 us
  transfers between devices with their start and end apart: 17, of which 12 were waited for; matrix products, arithmetic and copies ran while one was open for 21% of the time, Pallas kernels for 0%

commit v1 on v0

--- a/solution.py
+++ b/solution.py
@@ -3,6 +3,7 @@
 import jax.numpy as jnp
 from jax import lax
 from jax.sharding import PartitionSpec as P
+from jax.lax import all_gather
 
 HEAD = 64
 eps = 1e-05
@@ -202,7 +203,9 @@
 
     def reduce(v):
         v = v.reshape((n,) + v.shape[2:])
-        return lax.psum(lax.psum_scatter(v, RC, scatter_dimension=0, tiled=False), "dp")
+        return all_gather(
+            lax.psum_scatter(v, RC, scatter_dimension=0, tiled=False), axis_name="dp"
+        ).sum(axis=0)
 
     shr_w_g = reduce(d_shr_w).astype(f32)
     exp_w_g = reduce(d_exp_w).astype(f32)

time: 613 us -> 662 us (1.080)
  waiting for transfers between devices: 337 us -> 383 us
  other arithmetic: 45 us -> 52.1 us
    all_gather x0 -> x3, waiting for transfers between devices: none -> 115 us  [reduce(): all_gather(lax.psum_scatter(v, RC, scatter_dimension=0, tiled=False), axi...]
    psum x1 -> x0, waiting for transfers between devices: 38.6 us -> none  [reduce(): lax.psum(lax.psum_scatter(v, RC, scatter_dimension=0, tiled=False), 'dp')]
    all_to_all x2, waiting for transfers between devices: 42.4 us -> 18.2 us  [from_unit(): v = lax.all_to_all(v, 'dp', 0, 0, axis_index_groups=groups, tiled=True)]
    all_to_all x1 -> x0, blocking collectives: 20.6 us -> none  [from_unit(): v = lax.all_to_all(v.reshape(n, fl, unit), RC, 0, 0, tiled=True)]
    all_gather x0 -> x1, blocking collectives: none -> 20.6 us  [reduce(): all_gather(lax.psum_scatter(v, RC, scatter_dimension=0, tiled=False), axi...]
    reduce_scatter x4, waiting for transfers between devices: 133 us -> 116 us  [reduce(): lax.psum_scatter(v, RC, scatter_dimension=0, tiled=False)]
    all_to_all x1 -> x2, waiting for transfers between devices: 0.01 us -> 10.1 us  [from_unit(): v = lax.all_to_all(v.reshape(n, fl, unit), RC, 0, 0, tiled=True)]
    reduce_sum x0 -> x4, other arithmetic: none -> 6.74 us  [reduce(): return all_gather(lax.psum_scatter(v, RC, scatter_dimension=0, tiled=Fals...]
  transfers between devices with their start and end apart: 17 -> 20, of which waited for: 12 -> 15; matrix products, arithmetic and copies ran while one was open for 21% -> 18% of each run, Pallas kernels for 0% -> 0%
where the time goes in v1:
time: 662 us; the launch traced here: 656 us
  waiting for transfers between devices  383 us (58%)
  matrix products  93.7 us (14%)
  local copies, waits for them, and re-layouts  57.8 us (9%)
  other arithmetic  52.1 us (8%)
  starting transfers between devices  30.6 us (5%)
  blocking collectives  20.6 us (3%)
  between operations  17.9 us (3%)
    reduce_scatter x4, waiting for transfers between devices, reduce(): lax.psum_scatter(v, RC, scatter_dimension=0, tiled=False)  116 us
    all_gather x3, waiting for transfers between devices, reduce(): all_gather(lax.psum_scatter(v, RC, scatter_dimension=0, tiled=False), axi...  115 us
    all_gather x4, waiting for transfers between devices, gather(): return lax.all_gather(v, RC, axis=0)  88.5 us
    dot_general x17, matrix products, mm(): return jnp.einsum(spec, a, b, preferred_element_type=f32)  82.9 us
    unnamed x13, waiting for transfers between devices  20.7 us
    all_gather x1, blocking collectives, reduce(): all_gather(lax.psum_scatter(v, RC, scatter_dimension=0, tiled=False), axi...  20.6 us
    all_to_all x2, waiting for transfers between devices, from_unit(): v = lax.all_to_all(v, 'dp', 0, 0, axis_index_groups=groups, tiled=True)  18.2 us
    all_to_all x2, waiting for transfers between devices, to_unit(): v = lax.all_to_all(v, 'dp', 0, 0, axis_index_groups=groups, tiled=True)  14.4 us
  transfers between devices with their start and end apart: 20, of which 15 were waited for; matrix products, arithmetic and copies ran while one was open for 18% of the time, Pallas kernels for 0%

profile of v1, /device:TPU:0, one launch (start us, length us, event | category | flops | bytes accessed | tf_op | source)
XLA Modules:
  0.0 655.8 jit_solution(14088956415204731199)
XLA Ops:
  15.2 4.3 all-to-all-start
  20.6 10.5 %all-to-all-done = bf16[2,8,96,256]{3,1,2,0:T(8,128)(2,1)S(1)} async-done(((bf16[2,8,96,256]{3,1,2,0:T(8,128)(2,1)}), bf16[2,8,96,256]{3,1,2,0:T(8,128)(2,1)S(1)}, u32[]{:S(2)}, u32[]{:S(2)}) %all-to-all-start) | async-done | bytes 786464 | tf_op jit(solution)/shard_map/all_to_all | solution.py:84
  48.9 18.1 %all-reduce.4.cloned.1.call-done = f32[29184]{0:T(1024)} async-done(((f32[29184]{0:T(1024)}), f32[29184]{0:T(1024)}) %all-reduce.4.cloned.1.call-update) | async-done | bytes 116752
  73.6 4.2 all-to-all-start.5
  79.3 31.8 %all-gather.19.cloned.1.call-done = bf16[24,192,384]{2,1,0:T(8,128)(2,1)} async-done(((bf16[3,192,384]{2,1,0:T(8,128)(2,1)}), bf16[24,192,384]{2,1,0:T(8,128)(2,1)}) %all-gather.19.cloned.1.call-update) | async-done | bytes 3538960 | tf_op jit(solution)/shard_map/all_gather | solution.py:96
  117.5 10.8 %fusion.64 = (f32[12,512]{1,0:T(8,128)S(1)}, f32[12,512,512]{2,1,0:T(8,128)}) fusion(pred[512,512]{1,0:T(8,128)(4,1)S(1)} %broadcast_compare_fusion, bf16[12,64,512]{2,1,0:T(8,128)(2,1)S(1)} %bitcast.295, f32[12,64,512]{2,1,0:T(8,128)} %bitcast.298, f32[12,64]{1,0:T(8,128)S(1)} %add.252), kind=kOutput, calls=%fused_computation.139 | convolution fusion | flops 416023040 | bytes 15232000 | tf_op jit(solution)/shard_map/sub | solution.py:149
  128.3 6.6 fusion.65
  142.8 35.3 %all-gather.23.cloned.1.call-done = bf16[3072,768]{1,0:T(8,128)(2,1)} async-done(((bf16[384,768]{1,0:T(8,128)(2,1)}), bf16[3072,768]{1,0:T(8,128)(2,1)}) %all-gather.23.cloned.1.call-update) | async-done | bytes 4718608 | tf_op jit(solution)/shard_map/all_gather | solution.py:96
  178.1 9.2 %fusion.54 = (f32[512]{0:T(512)S(1)}, f32[4,768,512]{1,2,0:T(8,128)}, f32[4,768,512]{1,2,0:T(8,128)}) fusion(f32[4,768]{1,0:T(4,128)S(1)} %get-tuple-element.53, bf16[2,4,384,768]{3,2,1,0:T(8,128)(2,1)} %bitcast.336, f32[2,384]{1,0:T(2,128)S(1)} %add.267, f32[2,384]{1,0:T(2,128)S(1)} %mul.381, f32[512]{0:T(512)S(1)} %add_rsqrt_fusion.1, ...), kind=kOutput, calls=%fused_computation.130 | convolution fusion | flops 2427321856 | bytes 18898944 | tf_op jit(solution)/shard_map/rckn,rkt->cnt/dot_general | solution.py:17
  187.3 6.6 %copy.132 = f32[4,768,512]{2,1,0:T(8,128)} copy(f32[4,768,512]{1,2,0:T(8,128)} %get-tuple-element.75) | data formatting | bytes 12582912 | tf_op jit(solution)/shard_map/rckn,rkt->cnt/dot_general | solution.py:17
  197.5 21.4 %all-gather.25.cloned.1.call-done = bf16[6144,384]{1,0:T(8,128)(2,1)} async-done(((bf16[768,384]{1,0:T(8,128)(2,1)}), bf16[6144,384]{1,0:T(8,128)(2,1)}) %all-gather.25.cloned.1.call-update) | async-done | bytes 4718608 | tf_op jit(solution)/shard_map/all_gather | solution.py:96
  218.9 8.5 %fusion.8 = (bf16[3072]{0:T(1024)(128)(2,1)S(1)}, f32[512]{0:T(512)S(1)}, f32[512]{0:T(512)S(1)}, bf16[3072]{0:T(1024)(128)(2,1)S(1)}, f32[3072,512,1]{1,0,2:T(8,128)S(1)}) fusion(f32[4,768,512]{2,1,0:T(8,128)} %copy.132, f32[512]{0:T(512)S(1)} %broadcast_multiply_fusion.2, f32[3072]{0:T(1024)S(1)} %add.280, f32[512]{0:T(512)S(1)} %add_rsqrt_fusion, ...), kind=kOutput, calls=%fused_computation.17 | convolution fusion | flops 2437932032 | bytes 18132992 | tf_op jit(solution)/shard_map/rfd,rdt->ft/dot_general | solution.py:17
  227.5 7.7 %fusion.52 = (bf16[3072]{0:T(1024)(128)(2,1)S(1)}, bf16[3072,512]{1,0:T(8,128)(2,1)S(1)}) fusion(f32[512]{0:T(512)S(1)} %get-tuple-element.85, f32[512]{0:T(512)S(1)} %broadcast_multiply_fusion.2, f32[3072]{0:T(1024)S(1)} %add.280, f32[4,768,512]{2,1,0:T(8,128)S(1)} %bitcast.281, f32[512]{0:T(512)S(1)} %get-tuple-element.86, f32[3072]{0:T(1024)S(1)} %mul.396, ...), kind=kLoop, calls=%fused_computation.129 | loop fusion | flops 31454208 | bytes 15767552 | tf_op jit(solution)/shard_map/reduce_sum | solution.py:176
  235.2 6.0 fusion.30
  247.0 7.1 %fusion.67 = (bf16[12,64]{1,0:T(8,128)(2,1)S(1)}, bf16[12,64,512]{2,1,0:T(8,128)(2,1)S(1)}) fusion(bf16[12,64,512]{2,1,0:T(8,128)(2,1)} %bitcast.327, f32[12,512,512]{2,1,0:T(8,128)} %get-tuple-element.72, f32[12,512]{1,0:T(8,128)S(1)} %get-tuple-element.71), kind=kOutput, calls=%fused_computation.142 | convolution fusion | flops 409730304 | bytes 14181888 | tf_op jit(solution)/shard_map/heq,hkq->hek/dot_general | solution.py:17
  254.1 8.9 %multiply_reduce_fusion = (f32[12,512]{1,0:T(8,128)S(1)}, f32[12,512,512]{2,1,0:T(8,128)}) fusion(f32[12,512,512]{2,1,0:T(8,128)} %get-tuple-element.72, f32[12,512]{1,0:T(8,128)S(1)} %get-tuple-element.71, bf16[12,64,512]{2,1,0:T(8,128)(2,1)S(1)} %bitcast.328, f32[12,64,512]{2,1,0:T(8,128)S(1)} %bitcast.318, f32[12,64]{1,0:T(8,128)S(1)} %add.241), kind=kOutput, calls=%fused_computation.2 | convolution fusion | flops 412870656 | bytes 27577344 | tf_op jit(solution)/shard_map/hek,heq->hkq/dot_general | solution.py:17
  263.0 6.5 multiply_convert_fusion
  287.4 4.1 pad_maximum_fusion
  304.9 7.4 %convert_bitcast_fusion.1 = bf16[2,4,384,768]{2,3,0,1:T(8,128)(2,1)} fusion(bf16[4,768,512,1]{2,1,3,0:T(8,128)(2,1)} %bitcast.313, f32[2,384,512]{2,1,0:T(8,128)} %copy-done.9, f32[2,384]{1,0:T(2,128)S(1)} %add.267, f32[2,384]{1,0:T(2,128)S(1)} %mul.381, f32[512]{0:T(512)S(1)} %add_rsqrt_fusion.1, f32[512]{0:T(512)S(1)} %broadcast_multiply_fusion.9), kind=kOutput, calls=%fused_computation.30 | convolution fusion | flops 2420244480 | bytes 9447424 | tf_op jit(solution)/shard_map/rkt,cnt->rckn/dot_general | solution.py:17
  312.3 6.7 %copy.143 = bf16[2,4,384,768]{3,2,1,0:T(8,128)(2,1)} copy(bf16[2,4,384,768]{2,3,0,1:T(8,128)(2,1)} %convert_bitcast_fusion.1) | data formatting | bytes 9437184 | tf_op jit(solution)/shard_map/convert_element_type | solution.py:178
  321.9 18.5 %reduce-scatter.5.cloned.1.call-done = bf16[1,586,384]{2,1,0:T(8,128)(2,1)} async-done(((bf16[8,586,384]{2,1,0:T(8,128)(2,1)}), bf16[1,586,384]{2,1,0:T(8,128)(2,1)}) %reduce-scatter.5.cloned.1.call-update) | async-done | bytes 450064 | tf_op jit(solution)/shard_map/reduce_scatter | solution.py:207
  340.5 57.3 %reduce-scatter.11.cloned.1.call-done = bf16[1,768,384]{2,1,0:T(8,128)(2,1)} async-done(((bf16[8,768,384]{2,1,0:T(8,128)(2,1)}), bf16[1,768,384]{2,1,0:T(8,128)(2,1)}) %reduce-scatter.11.cloned.1.call-update) | async-done | bytes 589840 | tf_op jit(solution)/shard_map/reduce_scatter | solution.py:207
  397.8 4.7 copy.126
  402.5 5.7 fusion.69
  415.2 40.7 %reduce-scatter.9.cloned.1.call-done = bf16[1,384,768]{2,1,0:T(8,128)(2,1)} async-done(((bf16[8,384,768]{2,1,0:T(8,128)(2,1)}), bf16[1,384,768]{2,1,0:T(8,128)(2,1)}) %reduce-scatter.9.cloned.1.call-update) | async-done | bytes 589840 | tf_op jit(solution)/shard_map/reduce_scatter | solution.py:207
  461.0 10.1 %all-to-all-done.2 = bf16[8,96,512]{2,1,0:T(8,128)(2,1)S(1)} async-done(((bf16[8,96,512]{2,1,0:T(8,128)(2,1)}), bf16[8,96,512]{2,1,0:T(8,128)(2,1)S(1)}, u32[]{:S(2)}, u32[]{:S(2)}) %all-to-all-start.2) | async-done | bytes 786464 | tf_op jit(solution)/shard_map/all_to_all | solution.py:90
  476.1 9.3 %all-to-all-done.7 = bf16[2,8,96,256]{3,1,2,0:T(8,128)(2,1)S(1)} async-done(((bf16[2,8,96,256]{3,1,2,0:T(8,128)(2,1)}), bf16[2,8,96,256]{3,1,2,0:T(8,128)(2,1)S(1)}, u32[]{:S(2)}, u32[]{:S(2)}) %all-to-all-start.7) | async-done | bytes 786464 | tf_op jit(solution)/shard_map/all_to_all | solution.py:92
  490.3 8.8 %all-to-all-done.3 = bf16[2,8,96,256]{3,1,2,0:T(8,128)(2,1)S(1)} async-done(((bf16[2,8,96,256]{3,1,2,0:T(8,128)(2,1)}), bf16[2,8,96,256]{3,1,2,0:T(8,128)(2,1)S(1)}, u32[]{:S(2)}, u32[]{:S(2)}) %all-to-all-start.3) | async-done | bytes 786464 | tf_op jit(solution)/shard_map/all_to_all | solution.py:92
  500.3 20.6 %all_gather.53 = bf16[4,192,384]{2,1,0:T(8,128)(2,1)S(1)} all-gather(bf16[1,192,384]{2,1,0:T(8,128)(2,1)} %reduce-scatter.7.cloned.1.call-done), channel_id=1, replica_groups=mesh['dp'=4,'row'=2,'col'=4] {'dp'}, dimensions={0}, use_global_device_ids=true | all-gather | bytes 737280 | tf_op jit(solution)/shard_map/all_gather | solution.py:206
  521.8 22.3 %all-gather.13.cloned.1.call-done = bf16[4,586,384]{2,1,0:T(8,128)(2,1)} async-done(((bf16[1,586,384]{2,1,0:T(8,128)(2,1)}), bf16[4,586,384]{2,1,0:T(8,128)(2,1)}) %all-gather.13.cloned.1.call-update) | async-done | bytes 1800208 | tf_op jit(solution)/shard_map/all_gather | solution.py:206
  549.5 45.0 %all-gather.17.cloned.1.call-done = bf16[4,768,384]{2,1,0:T(8,128)(2,1)} async-done(((bf16[1,768,384]{2,1,0:T(8,128)(2,1)}), bf16[4,768,384]{2,1,0:T(8,128)(2,1)}) %all-gather.17.cloned.1.call-update) | async-done | bytes 2359312 | tf_op jit(solution)/shard_map/all_gather | solution.py:206
  597.9 47.4 %all-gather.15.cloned.1.call-done = bf16[4,384,768]{2,1,0:T(8,128)(2,1)} async-done(((bf16[1,384,768]{2,1,0:T(8,128)(2,1)}), bf16[4,384,768]{2,1,0:T(8,128)(2,1)}) %all-gather.15.cloned.1.call-update) | async-done | bytes 2359312 | tf_op jit(solution)/shard_map/all_gather | solution.py:206
  (273 shorter events, 125.9 us)
Async XLA Ops:
  7.2 31.3 %copy-start = (s32[8,4,4]{0,2,1:T(4,128)S(1)}, s32[8,4,4]{0,2,1:T(4,128)}, u32[]{:S(2)}) copy-start(s32[8,4,4]{0,2,1:T(4,128)} %param.23) | copy-start | bytes 1540
  7.2 59.8 %all-reduce.4.cloned.1.call-start = ((), (), s32[]{:S(2)}) async-start(), calls=%async_computation.23 | async-start | bytes 237568
  12.0 99.1 %all-gather.19.cloned.1.call-start = ((), (), s32[]{:S(2)}) async-start(), calls=%async_computation.19 | async-start | bytes 3981312 | tf_op jit(solution)/shard_map/all_gather | solution.py:96
  12.8 125.2 %all-gather.21.cloned.1.call-start = ((), (), s32[]{:S(2)}) async-start(), calls=%async_computation.20 | async-start | bytes 1327104 | tf_op jit(solution)/shard_map/all_gather | solution.py:96
  13.5 164.6 %all-gather.23.cloned.1.call-start = ((), (), s32[]{:S(2)}) async-start(), calls=%async_computation.21 | async-start | bytes 5308416 | tf_op jit(solution)/shard_map/all_gather | solution.py:96
  15.2 15.9 %all-to-all-start = ((bf16[2,8,96,256]{3,1,2,0:T(8,128)(2,1)}), bf16[2,8,96,256]{3,1,2,0:T(8,128)(2,1)S(1)}, u32[]{:S(2)}, u32[]{:S(2)}) async-start(bf16[2,8,96,256]{3,1,2,0:T(8,128)(2,1)} %copy.120), calls=%async_computation | async-start | bytes 1572864 | tf_op jit(solution)/shard_map/all_to_all | solution.py:84
  31.1 14.0 %all-to-all-start.4 = ((bf16[2,8,96,256]{3,1,2,0:T(8,128)(2,1)}), bf16[2,8,96,256]{3,1,2,0:T(8,128)(2,1)S(1)}, u32[]{:S(2)}, u32[]{:S(2)}) async-start(bf16[2,8,96,256]{3,1,2,0:T(8,128)(2,1)} %copy.130), calls=%async_computation.4 | async-start | bytes 1572864 | tf_op jit(solution)/shard_map/all_to_all | solution.py:84
  34.6 184.3 %all-gather.25.cloned.1.call-start = ((), (), s32[]{:S(2)}) async-start(), calls=%async_computation.22 | async-start | bytes 5308416 | tf_op jit(solution)/shard_map/all_gather | solution.py:96
  45.1 28.4 %all-to-all-start.1 = ((bf16[8,96,512]{2,1,0:T(8,128)(2,1)}), bf16[8,96,512]{2,1,0:T(8,128)(2,1)S(1)}, u32[]{:S(2)}, u32[]{:S(2)}) async-start(bf16[8,96,512]{2,1,0:T(8,128)(2,1)} %reshape.770), calls=%async_computation.1 | async-start | bytes 1572864 | tf_op jit(solution)/shard_map/all_to_all | solution.py:86
  69.7 9.1 %copy-start.42 = (f32[2,384]{1,0:T(2,128)}, f32[2,384]{1,0:T(2,128)S(1)}, u32[]{:S(2)}) copy-start(f32[2,384]{1,0:T(2,128)S(1)} %mul.364) | copy-start | bytes 9220
  73.6 123.9 %all-to-all-start.5 = ((bf16[8,96,512]{2,1,0:T(8,128)(2,1)}), bf16[8,96,512]{2,1,0:T(8,128)(2,1)}, u32[]{:S(2)}, u32[]{:S(2)}) async-start(bf16[8,96,512]{2,1,0:T(8,128)(2,1)} %reshape.782), calls=%async_computation.5 | async-start | bytes 1572864 | tf_op jit(solution)/shard_map/all_to_all | solution.py:86
  77.8 262.6 %reduce-scatter.5.cloned.1.call-start = ((), (), s32[]{:S(2)}) async-start(), calls=%async_computation.12 | async-start | bytes 4091904 | tf_op jit(solution)/shard_map/reduce_scatter | solution.py:207
  78.2 62.0 %copy-start.4 = (f32[8,96,512]{2,1,0:T(8,128)}, f32[8,96,512]{2,1,0:T(8,128)S(1)}, u32[]{:S(2)}) copy-start(f32[8,96,512]{2,1,0:T(8,128)S(1)} %convert_element_type.170) | copy-start | bytes 4718596
  78.7 36.5 %copy-start.40 = (f32[512]{0:T(512)}, f32[512]{0:T(512)S(1)}, u32[]{:S(2)}) copy-start(f32[512]{0:T(512)S(1)} %add_rsqrt_fusion.3) | copy-start | bytes 6148
  79.3 31.8 %copy-start.22 = (bf16[2,384,512,1,1]{2,1,4,3,0:T(8,128)(2,1)}, bf16[2,384,512,1,1]{2,1,4,3,0:T(8,128)(2,1)S(1)}, u32[]{:S(2)}) copy-start(bf16[2,384,512,1,1]{2,1,4,3,0:T(8,128)(2,1)S(1)} %fusion.41) | copy-start | bytes 2359300
  218.9 8.5 %slice-start = ((s8[6291456]{0:T(1024)(128)(4,1)}), s8[4194304]{0:T(1024)(128)(4,1)S(1)}, s32[]{:S(2)}) async-start(s8[6291456]{0:T(1024)(128)(4,1)} %bitcast.280), calls=%async_computation.24 | async-start | bytes 8388608
  218.9 8.5 %slice-start.1 = ((s8[6291456]{0:T(1024)(128)(4,1)}), s8[2097152]{0:T(1024)(128)(4,1)S(1)}, s32[]{:S(2)}) async-start(s8[6291456]{0:T(1024)(128)(4,1)} %bitcast.280), calls=%async_computation.25 | async-start | bytes 4194304
  227.5 7.7 %copy-start.10 = (f32[2,384,512]{2,1,0:T(8,128)S(1)}, f32[2,384,512]{2,1,0:T(8,128)}, u32[]{:S(2)}) copy-start(f32[2,384,512]{2,1,0:T(8,128)} %copy-done.9) | copy-start | bytes 4718596
  247.0 7.1 %copy-start.21 = (bf16[768,512]{1,0:T(8,128)(2,1)S(1)}, bf16[768,512]{1,0:T(8,128)(2,1)}, u32[]{:S(2)}) copy-start(bf16[768,512]{1,0:T(8,128)(2,1)} %copy.135) | copy-start | bytes 2359300
  247.0 16.0 %slice-start.2 = ((s8[12582912]{0:T(1024)(128)(4,1)}), s8[4194304]{0:T(1024)(128)(4,1)S(1)}, s32[]{:S(2)}) async-start(s8[12582912]{0:T(1024)(128)(4,1)} %bitcast.293), calls=%async_computation.26 | async-start | bytes 8388608
  247.0 16.0 %slice-start.3 = ((s8[12582912]{0:T(1024)(128)(4,1)}), s8[4194304]{0:T(1024)(128)(4,1)S(1)}, s32[]{:S(2)}) async-start(s8[12582912]{0:T(1024)(128)(4,1)} %bitcast.293), calls=%async_computation.27 | async-start | bytes 8388608
  254.1 8.9 %slice-start.4 = ((s8[12582912]{0:T(1024)(128)(4,1)}), s8[4194304]{0:T(1024)(128)(4,1)S(1)}, s32[]{:S(2)}) async-start(s8[12582912]{0:T(1024)(128)(4,1)} %bitcast.293), calls=%async_computation.28 | async-start | bytes 8388608
  291.6 106.2 %reduce-scatter.11.cloned.1.call-start = ((), (), s32[]{:S(2)}) async-start(), calls=%async_computation.17 | async-start | bytes 5308416 | tf_op jit(solution)/shard_map/reduce_scatter | solution.py:207
  304.7 151.2 %reduce-scatter.9.cloned.1.call-start = ((), (), s32[]{:S(2)}) async-start(), calls=%async_computation.15 | async-start | bytes 5308416 | tf_op jit(solution)/shard_map/reduce_scatter | solution.py:207
  319.0 181.3 %reduce-scatter.7.cloned.1.call-start = ((), (), s32[]{:S(2)}) async-start(), calls=%async_computation.14 | async-start | bytes 1327104 | tf_op jit(solution)/shard_map/reduce_scatter | solution.py:207
  321.9 222.2 %all-gather.13.cloned.1.call-start = ((), (), s32[]{:S(2)}) async-start(), calls=%async_computation.13 | async-start | bytes 2273280 | tf_op jit(solution)/shard_map/all_gather | solution.py:206
  340.5 254.0 %all-gather.17.cloned.1.call-start = ((), (), s32[]{:S(2)}) async-start(), calls=%async_computation.18 | async-start | bytes 2949120 | tf_op jit(solution)/shard_map/all_gather | solution.py:206
  411.6 44.3 %all-to-all-start.6 = ((bf16[8,96,512]{2,1,0:T(8,128)(2,1)}), bf16[8,96,512]{2,1,0:T(8,128)(2,1)S(1)}, u32[]{:S(2)}, u32[]{:S(2)}) async-start(bf16[8,96,512]{2,1,0:T(8,128)(2,1)} %get-tuple-element.43), calls=%async_computation.6 | async-start | bytes 1572864 | tf_op jit(solution)/shard_map/all_to_all | solution.py:90
  415.2 230.1 %all-gather.15.cloned.1.call-start = ((), (), s32[]{:S(2)}) async-start(), calls=%async_computation.16 | async-start | bytes 2949120 | tf_op jit(solution)/shard_map/all_gather | solution.py:206
  455.9 15.1 %all-to-all-start.2 = ((bf16[8,96,512]{2,1,0:T(8,128)(2,1)}), bf16[8,96,512]{2,1,0:T(8,128)(2,1)S(1)}, u32[]{:S(2)}, u32[]{:S(2)}) async-start(bf16[8,96,512]{2,1,0:T(8,128)(2,1)} %get-tuple-element.44), calls=%async_computation.2 | async-start | bytes 1572864 | tf_op jit(solution)/shard_map/all_to_all | solution.py:90
  471.1 14.4 %all-to-all-start.7 = ((bf16[2,8,96,256]{3,1,2,0:T(8,128)(2,1)}), bf16[2,8,96,256]{3,1,2,0:T(8,128)(2,1)S(1)}, u32[]{:S(2)}, u32[]{:S(2)}) async-start(bf16[2,8,96,256]{3,1,2,0:T(8,128)(2,1)} %copy.140), calls=%async_computation.7 | async-start | bytes 1572864 | tf_op jit(solution)/shard_map/all_to_all | solution.py:92
  485.5 13.6 %all-to-all-start.3 = ((bf16[2,8,96,256]{3,1,2,0:T(8,128)(2,1)}), bf16[2,8,96,256]{3,1,2,0:T(8,128)(2,1)S(1)}, u32[]{:S(2)}, u32[]{:S(2)}) async-start(bf16[2,8,96,256]{3,1,2,0:T(8,128)(2,1)} %copy.128), calls=%async_computation.3 | async-start | bytes 1572864 | tf_op jit(solution)/shard_map/all_to_all | solution.py:92
  (40 other events, 126.7 us)
Sparse Core Ops, SparseCore 0:
  12.1 54.8 all-reduce.3
  69.1 41.9 all-gather.18
  113.1 24.0 all-gather.20
  139.1 38.9 all-gather.22
  180.0 38.9 all-gather.24
  291.7 48.7 reduce-scatter.4
  343.9 53.8 reduce-scatter.10
  401.6 54.2 reduce-scatter.8
  459.7 36.7 reduce-scatter.6
  498.0 45.9 all-gather.12
  545.7 48.7 all-gather.16
  596.0 49.2 all-gather.14
